TPU v7x, 256 devices: a whole 4x4x8 slice. The times are simulated.
256 devices in a mesh: pipe: 8 (over x, y_hi), dp: 32 (over y_lo, z, core).
Axes of the slice: x: 4, y: 4 (y_hi: 2, y_lo: 2; y = y_hi * 2 + y_lo), z: 8, core: 2. Of those that a mesh axis runs over, the one named last changes fastest.
Arguments:
- tokens: bfloat16 [2, 64, 32, 4096], P(None, 'dp'), may hold values from -6 to 6
- cotangents: bfloat16 [2, 64, 32, 4096], P(None, 'dp'), may hold values from -1.5 to 1.5
- starts: int32 [2, 64, 4], P(None, 'dp'), may hold values from 0 to 31, as said below
- counts: int32 [2, 64], P(None, 'dp'), may hold values from 1 to 4
- layer_gains: bfloat16 [8, 4096], P('pipe', 'dp'), may hold values from 0.5 to 1.5
- first_map: bfloat16 [8, 4096, 128], P('pipe', 'dp'), may hold values from -0.09375 to 0.09375
- second_map: bfloat16 [8, 128, 4096], P('pipe', None, 'dp'), may hold values from -0.5 to 0.5
Outputs:
- gain_grad: float32 [8, 4096], P('pipe', 'dp')
- first_grad: float32 [8, 4096, 128], P('pipe', 'dp')
- second_grad: float32 [8, 128, 4096], P('pipe', None, 'dp')
Inputs may be any that keep to these rules, and one draw needn't show every extreme that they name: `starts`: each row begins with 0 and rises strictly; a micro-batch's documents begin at the first counts entries of its row, the later entries are not used.
All inputs are finite; a program needn't handle non-finite values.
Results may differ from a plain program's by a relative error of at most 0.03.
Values may be sent and summed in bfloat16 or wider, within the bound.
A program may use at most 64 MiB of HBM per device.

v0:
```python
import jax
import jax.numpy as jnp
from jax import lax
from jax.sharding import PartitionSpec as P

HD = 128


def partner(shard, axis, distance):
    return lax.ppermute(shard, axis, [(i, i ^ 1 << distance) for i in range(lax.axis_size(axis))])


def passed_along(value, axis, steps):
    count = lax.axis_size(axis)
    initial, last = (max(0, -steps), min(count, count - steps))
    return lax.ppermute(value, axis, [(source, source + steps) for source in range(initial, last)])


def shortened(shard):

    def short(part):
        return part.astype(jnp.bfloat16) if part.dtype == jnp.float32 else part

    return jax.tree.map(short, shard)


def doc_allowed(row_starts, row_count, length):
    positions = jnp.arange(length, dtype=jnp.int32)
    entries = jnp.arange(row_starts.shape[0], dtype=jnp.int32)
    started = (row_starts[None, :] <= positions[:, None]) & (entries < row_count)[None, :]
    document = jnp.sum(started.astype(jnp.int32), axis=1)
    matched = document[:, None] == document[None, :]
    return matched & (positions[None, :] <= positions[:, None])


def apply_layer(activation, gain_row, first_weight, second_weight, allowed):
    length = activation.shape[0]
    model_width = activation.shape[1]
    widened = activation.astype(jnp.float32)
    factor = lax.rsqrt(jnp.mean(widened * widened, axis=1, keepdims=True) + 1e-05)
    normed = (widened * factor * gain_row).astype(jnp.bfloat16)
    split_heads = normed.reshape(length, model_width // HD, HD)
    scores = (
        jnp.einsum("qhd,khd->hqk", split_heads, split_heads, preferred_element_type=jnp.float32)
        / HD
    )
    weights = jnp.where(allowed[None, :, :], jnp.exp(scores), 0.0)
    probabilities = (weights / jnp.sum(weights, axis=2, keepdims=True)).astype(jnp.bfloat16)
    mixed_heads = jnp.einsum(
        "hqk,khd->qhd", probabilities, split_heads, preferred_element_type=jnp.float32
    )
    mixed_heads = mixed_heads.reshape(length, model_width).astype(jnp.bfloat16)
    reduced = jnp.dot(mixed_heads, first_weight, preferred_element_type=jnp.float32).astype(
        jnp.bfloat16
    )
    return (widened + jnp.dot(reduced, second_weight, preferred_element_type=jnp.float32)).astype(
        jnp.bfloat16
    )


def layer_back(activation, gain_row, first_weight, second_weight, allowed, cotangent):
    _, pullback = jax.vjp(
        lambda act_in, gain_in, first_in, second_in: apply_layer(
            act_in, gain_in, first_in, second_in, allowed
        ),
        activation,
        gain_row,
        first_weight,
        second_weight,
    )
    return pullback(cotangent)


def add_masked(running_sums, gradients, live_flag):
    return tuple(
        (
            current + jnp.where(live_flag, gradient.astype(jnp.float32), 0.0)
            for current, gradient in zip(running_sums, gradients)
        )
    )


def round_parts(running_sums):
    return tuple(
        (lax.optimization_barrier(current.astype(jnp.bfloat16)) for current in running_sums)
    )


def per_device(tokens, cotangents, starts, counts, layer_gains, first_map, second_map):
    sections = lax.axis_size("pipe")
    my_section = lax.axis_index("pipe")
    bit_count = sections.bit_length() - 1
    micro_count = tokens.shape[1]
    length = tokens.shape[2]
    model_width = tokens.shape[3]
    tick_count = sections + micro_count - 1
    allowed_all = jax.vmap(
        jax.vmap(lambda row_starts, row_count: doc_allowed(row_starts, row_count, length))
    )(starts, counts)
    mirrored = (layer_gains, first_map, second_map)
    for bit_number in range(bit_count):
        mirrored = partner((mirrored[0], mirrored[1], mirrored[2]), "pipe", bit_number)
    stacked = (
        jnp.concatenate((layer_gains, mirrored[0]), axis=0),
        jnp.concatenate((first_map, mirrored[1]), axis=0),
        jnp.concatenate((second_map, mirrored[2]), axis=0),
    )
    full_gain, full_first, full_second = (
        lax.all_gather(stacked[0], "dp", axis=1, tiled=True),
        lax.all_gather(stacked[1], "dp", axis=1, tiled=True),
        lax.all_gather(stacked[2], "dp", axis=2, tiled=True),
    )

    def slot_of(index_value):
        live_flag = (index_value >= 0) & (index_value < micro_count)
        return (jnp.clip(index_value, 0, micro_count - 1), live_flag)

    def forward_tick(tick_index, loop_state):
        from_below, from_above, stashed = loop_state
        down_slot, down_live = slot_of(tick_index - my_section)
        up_slot, up_live = slot_of(tick_index - (sections - 1 - my_section))
        down_input = jnp.where(my_section == 0, tokens[0, down_slot], from_below)
        up_input = jnp.where(my_section == sections - 1, tokens[1, up_slot], from_above)
        down_output = apply_layer(
            down_input, full_gain[0], full_first[0], full_second[0], allowed_all[0, down_slot]
        )
        up_output = apply_layer(
            up_input, full_gain[1], full_first[1], full_second[1], allowed_all[1, up_slot]
        )
        stashed = stashed.at[0, down_slot].set(
            jnp.where(down_live, down_input, stashed[0, down_slot])
        )
        stashed = stashed.at[1, up_slot].set(jnp.where(up_live, up_input, stashed[1, up_slot]))
        from_below = passed_along(down_output, "pipe", 1)
        from_above = passed_along(up_output, "pipe", -1)
        return (from_below, from_above, stashed)

    empty_rows = jnp.zeros((length, model_width), jnp.bfloat16)
    empty_stash = jnp.zeros((2, micro_count, length, model_width), jnp.bfloat16)
    _, _, stashed = lax.fori_loop(
        0, tick_count, forward_tick, (empty_rows, empty_rows, empty_stash)
    )
    zero_sums = (
        jnp.zeros((model_width,), jnp.float32),
        jnp.zeros((model_width, first_map.shape[2]), jnp.float32),
        jnp.zeros((second_map.shape[1], model_width), jnp.float32),
    )

    def backward_tick(tick_index, loop_state):
        from_above, from_below, down_sums, up_sums = loop_state
        down_slot, down_live = slot_of(tick_index - (sections - 1 - my_section))
        up_slot, up_live = slot_of(tick_index - my_section)
        down_cot = jnp.where(my_section == sections - 1, cotangents[0, down_slot], from_above)
        up_cot = jnp.where(my_section == 0, cotangents[1, up_slot], from_below)
        down_back = layer_back(
            stashed[0, down_slot],
            full_gain[0],
            full_first[0],
            full_second[0],
            allowed_all[0, down_slot],
            down_cot,
        )
        up_back = layer_back(
            stashed[1, up_slot],
            full_gain[1],
            full_first[1],
            full_second[1],
            allowed_all[1, up_slot],
            up_cot,
        )
        down_sums = add_masked(down_sums, down_back[1:], down_live)
        up_sums = add_masked(up_sums, up_back[1:], up_live)
        from_above = passed_along(down_back[0], "pipe", -1)
        from_below = passed_along(up_back[0], "pipe", 1)
        return (from_above, from_below, down_sums, up_sums)

    _, _, down_sums, up_sums = lax.fori_loop(
        0, tick_count, backward_tick, (empty_rows, empty_rows, zero_sums, zero_sums)
    )
    down_parts = round_parts(down_sums)
    up_parts = round_parts(up_sums)
    received = up_parts
    for bit_number in range(bit_count):
        received = jax.tree.map(
            lambda part, own: part.astype(own.dtype),
            partner(shortened(received), "pipe", bit_number),
            received,
        )
    pair_sums = tuple(
        (
            own_part.astype(jnp.float32) + other_part.astype(jnp.float32)
            for own_part, other_part in zip(down_parts, received)
        )
    )
    gain_total, first_total, second_total = (
        lax.psum_scatter(
            pair_sums[0].astype(jnp.bfloat16), "dp", scatter_dimension=0, tiled=True
        ).astype(jnp.float32),
        lax.psum_scatter(
            pair_sums[1].astype(jnp.bfloat16), "dp", scatter_dimension=0, tiled=True
        ).astype(jnp.float32),
        lax.psum_scatter(
            pair_sums[2].astype(jnp.bfloat16), "dp", scatter_dimension=1, tiled=True
        ).astype(jnp.float32),
    )
    return (gain_total[None], first_total[None], second_total[None])


def solution(mesh):
    in_specs = (
        P(None, "dp", None, None),
        P(None, "dp", None, None),
        P(None, "dp", None),
        P(None, "dp"),
        P("pipe", "dp"),
        P("pipe", "dp", None),
        P("pipe", None, "dp"),
    )
    out_specs = (P("pipe", "dp"), P("pipe", "dp", None), P("pipe", None, "dp"))
    return jax.shard_map(
        per_device, mesh=mesh, in_specs=in_specs, out_specs=out_specs, check_vma=False
    )
```

profile of v0, /device:TPU:2, one launch (start us, length us, event | category | flops | bytes accessed | tf_op | source)
XLA Modules:
  0.0 1092.7 jit_solution(12410242168434772746)
XLA Ops:
  55.1 37.2 %all_gather.11 = bf16[2,4096]{1,0:T(2,128)(2,1)S(1)} all-gather(bf16[2,128]{1,0:T(2,128)(2,1)S(1)} %pad_maximum_fusion.2), channel_id=1, replica_groups=mesh['pipe'=8,'dp'=32] {'dp'}, dimensions={1}, use_global_device_ids=true | all-gather | bytes 16896 | tf_op jit(solution)/shard_map/all_gather | solution.py:109
  92.3 65.1 %all-gather.5.cloned.1.call-done = bf16[2,4096,128]{2,1,0:T(8,128)(2,1)} async-done(((bf16[2,128,128]{2,1,0:T(8,128)(2,1)}), bf16[2,4096,128]{2,1,0:T(8,128)(2,1)}) %all-gather.5.cloned.1.call-update) | async-done | bytes 2097168 | tf_op jit(solution)/shard_map/all_gather | solution.py:110
  158.2 282.0 %while.49 = (s32[]{:T(128)}, bf16[32,4096]{1,0:T(8,128)(2,1)S(1)}, bf16[32,4096]{1,0:T(8,128)(2,1)}, bf16[2,2,32,4096]{3,2,1,0:T(8,128)(2,1)S(1)}, pred[]{:T(512...) while((s32[]{:T(128)}, bf16[32,4096]{1,0:T(8,128)(2,1)S(1)}, ...), condition=%wide.region_8.9_spmd, body=%wide.region_1.8_spmd.sunk | while | flops 172771520 | bytes 23715560 | solution.py:140
  170.0 4.6 collective-permute-start.1
  183.5 9.9 collective-permute-done
  213.3 5.4 collective-permute-start
  218.7 6.4 collective-permute-done
  244.9 5.4 collective-permute-start
  250.4 5.5 collective-permute-done
  275.7 5.4 collective-permute-start
  281.2 5.4 collective-permute-done
  306.4 5.4 collective-permute-start
  311.9 5.4 collective-permute-done
  337.2 5.4 collective-permute-start
  342.6 5.4 collective-permute-done
  367.9 5.4 collective-permute-start
  373.3 5.4 collective-permute-done
  398.6 5.4 collective-permute-start
  404.1 5.4 collective-permute-done
  429.4 5.4 collective-permute-start
  434.8 5.4 collective-permute-done
  441.7 323.3 %while.50 = (s32[]{:T(128)}, bf16[32,4096]{1,0:T(8,128)(2,1)}, bf16[32,4096]{1,0:T(8,128)(2,1)}, f32[4096]{0:T(1024)S(1)}, f32[4096,128]{1,0:T(8,128)}, /*index=...) while((s32[]{:T(128)}, bf16[32,4096]{1,0:T(8,128)(2,1)}, ...), condition=%wide.region_20.21_spmd.clone, body=%wide.region_9.20_spmd.clone.sunk | while | flops 456771968 | bytes 73035120 | solution.py:177
  454.0 5.4 collective-permute-start.3
  487.5 4.5 collective-permute-start.3
  495.2 3.9 fusion.335
  502.5 3.7 fusion.338
  523.9 4.5 collective-permute-start.3
  531.6 3.9 fusion.335
  538.9 3.7 fusion.338
  556.7 3.7 collective-permute-start.2
  560.4 4.5 collective-permute-start.3
  568.0 3.9 fusion.335
  575.4 3.7 fusion.338
  593.1 3.7 collective-permute-start.2
  596.8 4.5 collective-permute-start.3
  604.5 3.9 fusion.335
  611.8 3.7 fusion.338
  629.6 3.7 collective-permute-start.2
  633.3 4.5 collective-permute-start.3
  640.9 3.9 fusion.335
  648.3 3.7 fusion.338
  666.0 3.7 collective-permute-start.2
  669.7 4.5 collective-permute-start.3
  677.4 3.9 fusion.335
  684.7 3.7 fusion.338
  706.2 4.5 collective-permute-start.3
  713.8 3.9 fusion.335
  721.2 3.7 fusion.338
  738.9 3.7 collective-permute-start.2
  742.6 4.5 collective-permute-start.3
  750.3 3.9 fusion.335
  757.6 3.7 fusion.338
  766.8 4.5 collective-permute-start.19
  771.3 19.6 %collective-permute-done.19 = bf16[128,4096]{1,0:T(8,128)(2,1)S(1)} collective-permute-done((bf16[128,4096]{1,0:T(8,128)(2,1)S(1)}, bf16[128,4096]{1,0:T(8,128)(2,1)S(1)}, u32[]{:S(2)}, u32[]{:S(2)}) %collective-permute-start.19) | collective-permute-done | bytes 1048608 | tf_op jit(solution)/shard_map/ppermute | solution.py:10
  791.0 4.0 collective-permute-start.16
  795.1 21.9 %collective-permute-done.20 = bf16[128,4096]{1,0:T(8,128)(2,1)S(1)} collective-permute-done((bf16[128,4096]{1,0:T(8,128)(2,1)S(1)}, bf16[128,4096]{1,0:T(8,128)(2,1)S(1)}, u32[]{:S(2)}, u32[]{:S(2)}) %collective-permute-start.20) | collective-permute-done | bytes 1048608 | tf_op jit(solution)/shard_map/ppermute | solution.py:10
  816.9 7.6 collective-permute-start.21
  825.4 19.1 %collective-permute-done.21 = bf16[128,4096]{1,0:T(8,128)(2,1)S(1)} collective-permute-done((bf16[128,4096]{1,0:T(8,128)(2,1)S(1)}, bf16[128,4096]{1,0:T(8,128)(2,1)S(1)}, u32[]{:S(2)}, u32[]{:S(2)}) %collective-permute-start.21) | collective-permute-done | bytes 1048608 | tf_op jit(solution)/shard_map/ppermute | solution.py:10
  848.3 13.1 %collective-permute-done.17 = bf16[4096,128]{1,0:T(8,128)(2,1)} collective-permute-done((bf16[4096,128]{1,0:T(8,128)(2,1)}, bf16[4096,128]{1,0:T(8,128)(2,1)}, u32[]{:S(2)}, u32[]{:S(2)}) %collective-permute-start.17) | collective-permute-done | bytes 1048608 | tf_op jit(solution)/shard_map/ppermute | solution.py:10
  861.5 16.5 %collective-permute-done.18 = bf16[4096,128]{1,0:T(8,128)(2,1)S(1)} collective-permute-done((bf16[4096,128]{1,0:T(8,128)(2,1)}, bf16[4096,128]{1,0:T(8,128)(2,1)S(1)}, u32[]{:S(2)}, u32[]{:S(2)}) %collective-permute-start.18) | collective-permute-done | bytes 1048608 | tf_op jit(solution)/shard_map/ppermute | solution.py:10
  889.5 3.9 collective-permute-done.15
  893.4 54.2 %all-reduce = bf16[4096]{0:T(1024)(128)(2,1)S(1)} all-reduce(bf16[4096]{0:T(1024)(128)(2,1)S(1)} %add_convert_fusion.2), channel_id=2, replica_groups=mesh['pipe'=8,'dp'=32] {'dp'}, use_global_device_ids=true, to_apply=%region_21.22.clone | all-reduce | flops 4096 | bytes 16384
  948.2 20.0 %reduce-scatter.7.cloned.1.call-done = bf16[128,128]{1,0:T(8,128)(2,1)} async-done(((bf16[4096,128]{1,0:T(8,128)(2,1)}), bf16[128,128]{1,0:T(8,128)(2,1)}) %reduce-scatter.7.cloned.1.call-update) | async-done | bytes 32784
  969.7 115.0 %reduce-scatter.5.cloned.1.call-done = bf16[128,128]{1,0:T(8,128)(2,1)} async-done(((bf16[4096,128]{1,0:T(8,128)(2,1)}), bf16[128,128]{1,0:T(8,128)(2,1)}) %reduce-scatter.5.cloned.1.call-update) | async-done | bytes 32784 | tf_op jit(solution)/shard_map/reduce_scatter | solution.py:199
  (767 shorter events, 449.4 us)
Async XLA Ops:
  7.2 85.1 %all-gather.3.cloned.1.call-start = ((), (), s32[]{:S(2)}) async-start(), calls=%async_computation.2 | async-start | bytes 2162688 | tf_op jit(solution)/shard_map/all_gather | solution.py:111
  7.2 5.7 collective-permute-start.4
  12.9 4.1 collective-permute-start.5
  17.1 5.4 collective-permute-start.6
  23.9 133.4 %all-gather.5.cloned.1.call-start = ((), (), s32[]{:S(2)}) async-start(), calls=%async_computation.3 | async-start | bytes 2162688 | tf_op jit(solution)/shard_map/all_gather | solution.py:110
  23.9 5.7 collective-permute-start.7
  29.7 3.9 collective-permute-start.8
  33.6 5.4 collective-permute-start.9
  40.4 927.8 %reduce-scatter.7.cloned.1.call-start = ((), (), s32[]{:S(2)}) async-start(), calls=%async_computation.5 | async-start | bytes 1081344
  40.5 5.3 collective-permute-start.10
  45.8 3.6 collective-permute-start.11
  49.3 5.1 collective-permute-start.12
  170.0 13.5 %collective-permute-start.1 = (bf16[32,4096]{1,0:T(8,128)(2,1)}, bf16[32,4096]{1,0:T(8,128)(2,1)}, u32[]{:S(2)}, u32[]{:S(2)}) collective-permute-start(bf16[32,4096]{1,0:T(8,128)(2,1)} %fusion.286), channel_id=1, source_target_pairs={{32,0},{64,32},{96,64},{128,96},{160,128},{192,160},{224,192},{33,... | collective-permute-start | bytes 786440 | tf_op jit(solution)/shard_map/while/body/eval_jaxpr/ppermute | solution.py:16
  180.8 12.6 %collective-permute-start = (bf16[32,4096]{1,0:T(8,128)(2,1)}, bf16[32,4096]{1,0:T(8,128)(2,1)S(1)}, u32[]{:S(2)}, u32[]{:S(2)}) collective-permute-start(bf16[32,4096]{1,0:T(8,128)(2,1)} %fusion.281), channel_id=1, source_target_pairs={{0,32},{32,64},{64,96},{96,128},{128,160},{160,192},{192,224},{1,3... | collective-permute-start | bytes 786440 | tf_op jit(solution)/shard_map/while/body/eval_jaxpr/ppermute | solution.py:16
  205.2 13.5 %collective-permute-start.1 = (bf16[32,4096]{1,0:T(8,128)(2,1)}, bf16[32,4096]{1,0:T(8,128)(2,1)}, u32[]{:S(2)}, u32[]{:S(2)}) collective-permute-start(bf16[32,4096]{1,0:T(8,128)(2,1)} %fusion.286), channel_id=1, source_target_pairs={{32,0},{64,32},{96,64},{128,96},{160,128},{192,160},{224,192},{33,... | collective-permute-start | bytes 786440 | tf_op jit(solution)/shard_map/while/body/eval_jaxpr/ppermute | solution.py:16
  213.3 11.8 %collective-permute-start = (bf16[32,4096]{1,0:T(8,128)(2,1)}, bf16[32,4096]{1,0:T(8,128)(2,1)S(1)}, u32[]{:S(2)}, u32[]{:S(2)}) collective-permute-start(bf16[32,4096]{1,0:T(8,128)(2,1)} %fusion.281), channel_id=1, source_target_pairs={{0,32},{32,64},{64,96},{96,128},{128,160},{160,192},{192,224},{1,3... | collective-permute-start | bytes 786440 | tf_op jit(solution)/shard_map/while/body/eval_jaxpr/ppermute | solution.py:16
  236.9 13.5 %collective-permute-start.1 = (bf16[32,4096]{1,0:T(8,128)(2,1)}, bf16[32,4096]{1,0:T(8,128)(2,1)}, u32[]{:S(2)}, u32[]{:S(2)}) collective-permute-start(bf16[32,4096]{1,0:T(8,128)(2,1)} %fusion.286), channel_id=1, source_target_pairs={{32,0},{64,32},{96,64},{128,96},{160,128},{192,160},{224,192},{33,... | collective-permute-start | bytes 786440 | tf_op jit(solution)/shard_map/while/body/eval_jaxpr/ppermute | solution.py:16
  244.9 10.9 %collective-permute-start = (bf16[32,4096]{1,0:T(8,128)(2,1)}, bf16[32,4096]{1,0:T(8,128)(2,1)S(1)}, u32[]{:S(2)}, u32[]{:S(2)}) collective-permute-start(bf16[32,4096]{1,0:T(8,128)(2,1)} %fusion.281), channel_id=1, source_target_pairs={{0,32},{32,64},{64,96},{96,128},{128,160},{160,192},{192,224},{1,3... | collective-permute-start | bytes 786440 | tf_op jit(solution)/shard_map/while/body/eval_jaxpr/ppermute | solution.py:16
  267.7 13.5 %collective-permute-start.1 = (bf16[32,4096]{1,0:T(8,128)(2,1)}, bf16[32,4096]{1,0:T(8,128)(2,1)}, u32[]{:S(2)}, u32[]{:S(2)}) collective-permute-start(bf16[32,4096]{1,0:T(8,128)(2,1)} %fusion.286), channel_id=1, source_target_pairs={{32,0},{64,32},{96,64},{128,96},{160,128},{192,160},{224,192},{33,... | collective-permute-start | bytes 786440 | tf_op jit(solution)/shard_map/while/body/eval_jaxpr/ppermute | solution.py:16
  275.7 10.9 collective-permute-start
  298.4 13.5 %collective-permute-start.1 = (bf16[32,4096]{1,0:T(8,128)(2,1)}, bf16[32,4096]{1,0:T(8,128)(2,1)}, u32[]{:S(2)}, u32[]{:S(2)}) collective-permute-start(bf16[32,4096]{1,0:T(8,128)(2,1)} %fusion.286), channel_id=1, source_target_pairs={{32,0},{64,32},{96,64},{128,96},{160,128},{192,160},{224,192},{33,... | collective-permute-start | bytes 786440 | tf_op jit(solution)/shard_map/while/body/eval_jaxpr/ppermute | solution.py:16
  306.4 10.9 collective-permute-start
  329.1 13.5 %collective-permute-start.1 = (bf16[32,4096]{1,0:T(8,128)(2,1)}, bf16[32,4096]{1,0:T(8,128)(2,1)}, u32[]{:S(2)}, u32[]{:S(2)}) collective-permute-start(bf16[32,4096]{1,0:T(8,128)(2,1)} %fusion.286), channel_id=1, source_target_pairs={{32,0},{64,32},{96,64},{128,96},{160,128},{192,160},{224,192},{33,... | collective-permute-start | bytes 786440 | tf_op jit(solution)/shard_map/while/body/eval_jaxpr/ppermute | solution.py:16
  337.2 10.9 collective-permute-start
  359.9 13.5 %collective-permute-start.1 = (bf16[32,4096]{1,0:T(8,128)(2,1)}, bf16[32,4096]{1,0:T(8,128)(2,1)}, u32[]{:S(2)}, u32[]{:S(2)}) collective-permute-start(bf16[32,4096]{1,0:T(8,128)(2,1)} %fusion.286), channel_id=1, source_target_pairs={{32,0},{64,32},{96,64},{128,96},{160,128},{192,160},{224,192},{33,... | collective-permute-start | bytes 786440 | tf_op jit(solution)/shard_map/while/body/eval_jaxpr/ppermute | solution.py:16
  367.9 10.9 collective-permute-start
  390.6 13.5 %collective-permute-start.1 = (bf16[32,4096]{1,0:T(8,128)(2,1)}, bf16[32,4096]{1,0:T(8,128)(2,1)}, u32[]{:S(2)}, u32[]{:S(2)}) collective-permute-start(bf16[32,4096]{1,0:T(8,128)(2,1)} %fusion.286), channel_id=1, source_target_pairs={{32,0},{64,32},{96,64},{128,96},{160,128},{192,160},{224,192},{33,... | collective-permute-start | bytes 786440 | tf_op jit(solution)/shard_map/while/body/eval_jaxpr/ppermute | solution.py:16
  398.6 10.9 collective-permute-start
  421.3 13.5 %collective-permute-start.1 = (bf16[32,4096]{1,0:T(8,128)(2,1)}, bf16[32,4096]{1,0:T(8,128)(2,1)}, u32[]{:S(2)}, u32[]{:S(2)}) collective-permute-start(bf16[32,4096]{1,0:T(8,128)(2,1)} %fusion.286), channel_id=1, source_target_pairs={{32,0},{64,32},{96,64},{128,96},{160,128},{192,160},{224,192},{33,... | collective-permute-start | bytes 786440 | tf_op jit(solution)/shard_map/while/body/eval_jaxpr/ppermute | solution.py:16
  429.4 10.9 collective-permute-start
  444.8 6.4 copy-start.3
  452.1 22.1 %collective-permute-start.2 = (bf16[32,4096]{1,0:T(8,128)(2,1)}, bf16[32,4096]{1,0:T(8,128)(2,1)}, u32[]{:S(2)}, u32[]{:S(2)}) collective-permute-start(bf16[32,4096]{1,0:T(8,128)(2,1)} %fusion.332), channel_id=1, source_target_pairs={{32,0},{64,32},{96,64},{128,96},{160,128},{192,160},{224,192},{33,... | collective-permute-start | bytes 786440 | tf_op jit(solution)/shard_map/while/body/eval_jaxpr/ppermute | solution.py:16
  454.0 20.2 %collective-permute-start.3 = (bf16[32,4096]{1,0:T(8,128)(2,1)}, bf16[32,4096]{1,0:T(8,128)(2,1)}, u32[]{:S(2)}, u32[]{:S(2)}) collective-permute-start(bf16[32,4096]{1,0:T(8,128)(2,1)} %get-tuple-element.1028), channel_id=1, source_target_pairs={{0,32},{32,64},{64,96},{96,128},{128,160},{160,192},{192,224},{1,3... | collective-permute-start | bytes 786440 | tf_op jit(solution)/shard_map/while/body/eval_jaxpr/ppermute | solution.py:16
  477.4 6.4 copy-start.3
  484.7 25.1 %collective-permute-start.2 = (bf16[32,4096]{1,0:T(8,128)(2,1)}, bf16[32,4096]{1,0:T(8,128)(2,1)}, u32[]{:S(2)}, u32[]{:S(2)}) collective-permute-start(bf16[32,4096]{1,0:T(8,128)(2,1)} %fusion.332), channel_id=1, source_target_pairs={{32,0},{64,32},{96,64},{128,96},{160,128},{192,160},{224,192},{33,... | collective-permute-start | bytes 786440 | tf_op jit(solution)/shard_map/while/body/eval_jaxpr/ppermute | solution.py:16
  487.5 22.3 %collective-permute-start.3 = (bf16[32,4096]{1,0:T(8,128)(2,1)}, bf16[32,4096]{1,0:T(8,128)(2,1)}, u32[]{:S(2)}, u32[]{:S(2)}) collective-permute-start(bf16[32,4096]{1,0:T(8,128)(2,1)} %get-tuple-element.1028), channel_id=1, source_target_pairs={{0,32},{32,64},{64,96},{96,128},{128,160},{160,192},{192,224},{1,3... | collective-permute-start | bytes 786440 | tf_op jit(solution)/shard_map/while/body/eval_jaxpr/ppermute | solution.py:16
  520.2 26.0 %collective-permute-start.2 = (bf16[32,4096]{1,0:T(8,128)(2,1)}, bf16[32,4096]{1,0:T(8,128)(2,1)}, u32[]{:S(2)}, u32[]{:S(2)}) collective-permute-start(bf16[32,4096]{1,0:T(8,128)(2,1)} %fusion.332), channel_id=1, source_target_pairs={{32,0},{64,32},{96,64},{128,96},{160,128},{192,160},{224,192},{33,... | collective-permute-start | bytes 786440 | tf_op jit(solution)/shard_map/while/body/eval_jaxpr/ppermute | solution.py:16
  523.9 22.3 %collective-permute-start.3 = (bf16[32,4096]{1,0:T(8,128)(2,1)}, bf16[32,4096]{1,0:T(8,128)(2,1)}, u32[]{:S(2)}, u32[]{:S(2)}) collective-permute-start(bf16[32,4096]{1,0:T(8,128)(2,1)} %get-tuple-element.1028), channel_id=1, source_target_pairs={{0,32},{32,64},{64,96},{96,128},{128,160},{160,192},{192,224},{1,3... | collective-permute-start | bytes 786440 | tf_op jit(solution)/shard_map/while/body/eval_jaxpr/ppermute | solution.py:16
  556.7 26.0 %collective-permute-start.2 = (bf16[32,4096]{1,0:T(8,128)(2,1)}, bf16[32,4096]{1,0:T(8,128)(2,1)}, u32[]{:S(2)}, u32[]{:S(2)}) collective-permute-start(bf16[32,4096]{1,0:T(8,128)(2,1)} %fusion.332), channel_id=1, source_target_pairs={{32,0},{64,32},{96,64},{128,96},{160,128},{192,160},{224,192},{33,... | collective-permute-start | bytes 786440 | tf_op jit(solution)/shard_map/while/body/eval_jaxpr/ppermute | solution.py:16
  560.4 22.3 %collective-permute-start.3 = (bf16[32,4096]{1,0:T(8,128)(2,1)}, bf16[32,4096]{1,0:T(8,128)(2,1)}, u32[]{:S(2)}, u32[]{:S(2)}) collective-permute-start(bf16[32,4096]{1,0:T(8,128)(2,1)} %get-tuple-element.1028), channel_id=1, source_target_pairs={{0,32},{32,64},{64,96},{96,128},{128,160},{160,192},{192,224},{1,3... | collective-permute-start | bytes 786440 | tf_op jit(solution)/shard_map/while/body/eval_jaxpr/ppermute | solution.py:16
  593.1 26.0 %collective-permute-start.2 = (bf16[32,4096]{1,0:T(8,128)(2,1)}, bf16[32,4096]{1,0:T(8,128)(2,1)}, u32[]{:S(2)}, u32[]{:S(2)}) collective-permute-start(bf16[32,4096]{1,0:T(8,128)(2,1)} %fusion.332), channel_id=1, source_target_pairs={{32,0},{64,32},{96,64},{128,96},{160,128},{192,160},{224,192},{33,... | collective-permute-start | bytes 786440 | tf_op jit(solution)/shard_map/while/body/eval_jaxpr/ppermute | solution.py:16
  596.8 22.3 %collective-permute-start.3 = (bf16[32,4096]{1,0:T(8,128)(2,1)}, bf16[32,4096]{1,0:T(8,128)(2,1)}, u32[]{:S(2)}, u32[]{:S(2)}) collective-permute-start(bf16[32,4096]{1,0:T(8,128)(2,1)} %get-tuple-element.1028), channel_id=1, source_target_pairs={{0,32},{32,64},{64,96},{96,128},{128,160},{160,192},{192,224},{1,3... | collective-permute-start | bytes 786440 | tf_op jit(solution)/shard_map/while/body/eval_jaxpr/ppermute | solution.py:16
  629.6 26.0 %collective-permute-start.2 = (bf16[32,4096]{1,0:T(8,128)(2,1)}, bf16[32,4096]{1,0:T(8,128)(2,1)}, u32[]{:S(2)}, u32[]{:S(2)}) collective-permute-start(bf16[32,4096]{1,0:T(8,128)(2,1)} %fusion.332), channel_id=1, source_target_pairs={{32,0},{64,32},{96,64},{128,96},{160,128},{192,160},{224,192},{33,... | collective-permute-start | bytes 786440 | tf_op jit(solution)/shard_map/while/body/eval_jaxpr/ppermute | solution.py:16
  633.3 22.3 %collective-permute-start.3 = (bf16[32,4096]{1,0:T(8,128)(2,1)}, bf16[32,4096]{1,0:T(8,128)(2,1)}, u32[]{:S(2)}, u32[]{:S(2)}) collective-permute-start(bf16[32,4096]{1,0:T(8,128)(2,1)} %get-tuple-element.1028), channel_id=1, source_target_pairs={{0,32},{32,64},{64,96},{96,128},{128,160},{160,192},{192,224},{1,3... | collective-permute-start | bytes 786440 | tf_op jit(solution)/shard_map/while/body/eval_jaxpr/ppermute | solution.py:16
  666.0 26.0 %collective-permute-start.2 = (bf16[32,4096]{1,0:T(8,128)(2,1)}, bf16[32,4096]{1,0:T(8,128)(2,1)}, u32[]{:S(2)}, u32[]{:S(2)}) collective-permute-start(bf16[32,4096]{1,0:T(8,128)(2,1)} %fusion.332), channel_id=1, source_target_pairs={{32,0},{64,32},{96,64},{128,96},{160,128},{192,160},{224,192},{33,... | collective-permute-start | bytes 786440 | tf_op jit(solution)/shard_map/while/body/eval_jaxpr/ppermute | solution.py:16
  669.7 22.3 %collective-permute-start.3 = (bf16[32,4096]{1,0:T(8,128)(2,1)}, bf16[32,4096]{1,0:T(8,128)(2,1)}, u32[]{:S(2)}, u32[]{:S(2)}) collective-permute-start(bf16[32,4096]{1,0:T(8,128)(2,1)} %get-tuple-element.1028), channel_id=1, source_target_pairs={{0,32},{32,64},{64,96},{96,128},{128,160},{160,192},{192,224},{1,3... | collective-permute-start | bytes 786440 | tf_op jit(solution)/shard_map/while/body/eval_jaxpr/ppermute | solution.py:16
  702.5 26.0 %collective-permute-start.2 = (bf16[32,4096]{1,0:T(8,128)(2,1)}, bf16[32,4096]{1,0:T(8,128)(2,1)}, u32[]{:S(2)}, u32[]{:S(2)}) collective-permute-start(bf16[32,4096]{1,0:T(8,128)(2,1)} %fusion.332), channel_id=1, source_target_pairs={{32,0},{64,32},{96,64},{128,96},{160,128},{192,160},{224,192},{33,... | collective-permute-start | bytes 786440 | tf_op jit(solution)/shard_map/while/body/eval_jaxpr/ppermute | solution.py:16
  706.2 22.3 %collective-permute-start.3 = (bf16[32,4096]{1,0:T(8,128)(2,1)}, bf16[32,4096]{1,0:T(8,128)(2,1)}, u32[]{:S(2)}, u32[]{:S(2)}) collective-permute-start(bf16[32,4096]{1,0:T(8,128)(2,1)} %get-tuple-element.1028), channel_id=1, source_target_pairs={{0,32},{32,64},{64,96},{96,128},{128,160},{160,192},{192,224},{1,3... | collective-permute-start | bytes 786440 | tf_op jit(solution)/shard_map/while/body/eval_jaxpr/ppermute | solution.py:16
  738.9 26.0 %collective-permute-start.2 = (bf16[32,4096]{1,0:T(8,128)(2,1)}, bf16[32,4096]{1,0:T(8,128)(2,1)}, u32[]{:S(2)}, u32[]{:S(2)}) collective-permute-start(bf16[32,4096]{1,0:T(8,128)(2,1)} %fusion.332), channel_id=1, source_target_pairs={{32,0},{64,32},{96,64},{128,96},{160,128},{192,160},{224,192},{33,... | collective-permute-start | bytes 786440 | tf_op jit(solution)/shard_map/while/body/eval_jaxpr/ppermute | solution.py:16
  742.6 22.3 %collective-permute-start.3 = (bf16[32,4096]{1,0:T(8,128)(2,1)}, bf16[32,4096]{1,0:T(8,128)(2,1)}, u32[]{:S(2)}, u32[]{:S(2)}) collective-permute-start(bf16[32,4096]{1,0:T(8,128)(2,1)} %get-tuple-element.1028), channel_id=1, source_target_pairs={{0,32},{32,64},{64,96},{96,128},{128,160},{160,192},{192,224},{1,3... | collective-permute-start | bytes 786440 | tf_op jit(solution)/shard_map/while/body/eval_jaxpr/ppermute | solution.py:16
  764.9 26.0 %copy-start.7 = (f32[4096,128]{1,0:T(8,128)S(1)}, f32[4096,128]{1,0:T(8,128)}, u32[]{:S(2)}) copy-start(f32[4096,128]{1,0:T(8,128)} %get-tuple-element.610) | copy-start | bytes 6291460
  766.8 57.8 %copy-start.5 = (f32[128,4096]{1,0:T(8,128)S(1)}, f32[128,4096]{1,0:T(8,128)}, u32[]{:S(2)}) copy-start(f32[128,4096]{1,0:T(8,128)} %get-tuple-element.611) | copy-start | bytes 6291460
  766.8 24.1 %collective-permute-start.19 = (bf16[128,4096]{1,0:T(8,128)(2,1)S(1)}, bf16[128,4096]{1,0:T(8,128)(2,1)S(1)}, u32[]{:S(2)}, u32[]{:S(2)}) collective-permute-start(bf16[128,4096]{1,0:T(8,128)(2,1)S(1)} %convert_element_type.624), channel_id=1, source_target_pairs={{0,32},{32,0},{64,96},{96,64},{128,160},{160,128},{192,224},{224,1... | collective-permute-start | bytes 3145736 | tf_op jit(solution)/shard_map/ppermute | solution.py:10
  790.9 26.0 %collective-permute-start.20 = (bf16[128,4096]{1,0:T(8,128)(2,1)S(1)}, bf16[128,4096]{1,0:T(8,128)(2,1)S(1)}, u32[]{:S(2)}, u32[]{:S(2)}) collective-permute-start(bf16[128,4096]{1,0:T(8,128)(2,1)S(1)} %collective-permute-done.19), channel_id=1, source_target_pairs={{0,64},{32,96},{64,0},{96,32},{128,192},{160,224},{192,128},{224,1... | collective-permute-start | bytes 3145736 | tf_op jit(solution)/shard_map/ppermute | solution.py:10
  791.0 33.7 %collective-permute-start.16 = (bf16[4096,128]{1,0:T(8,128)(2,1)S(1)}, bf16[4096,128]{1,0:T(8,128)(2,1)}, u32[]{:S(2)}, u32[]{:S(2)}) collective-permute-start(bf16[4096,128]{1,0:T(8,128)(2,1)S(1)} %convert_element_type.619), channel_id=1, source_target_pairs={{0,32},{32,0},{64,96},{96,64},{128,160},{160,128},{192,224},{224,1... | collective-permute-start | bytes 3145736 | tf_op jit(solution)/shard_map/ppermute | solution.py:10
  816.9 27.6 %collective-permute-start.21 = (bf16[128,4096]{1,0:T(8,128)(2,1)S(1)}, bf16[128,4096]{1,0:T(8,128)(2,1)S(1)}, u32[]{:S(2)}, u32[]{:S(2)}) collective-permute-start(bf16[128,4096]{1,0:T(8,128)(2,1)S(1)} %collective-permute-done.20), channel_id=1, source_target_pairs={{0,128},{32,160},{64,192},{96,224},{128,0},{160,32},{192,64},{224,... | collective-permute-start | bytes 3145736 | tf_op jit(solution)/shard_map/ppermute | solution.py:10
  824.7 36.7 %collective-permute-start.17 = (bf16[4096,128]{1,0:T(8,128)(2,1)}, bf16[4096,128]{1,0:T(8,128)(2,1)}, u32[]{:S(2)}, u32[]{:S(2)}) collective-permute-start(bf16[4096,128]{1,0:T(8,128)(2,1)} %collective-permute-done.16), channel_id=1, source_target_pairs={{0,64},{32,96},{64,0},{96,32},{128,192},{160,224},{192,128},{224,1... | collective-permute-start | bytes 3145736 | tf_op jit(solution)/shard_map/ppermute | solution.py:10
  845.8 15.6 %copy-start.6 = (f32[4096,128]{1,0:T(8,128)S(1)}, f32[4096,128]{1,0:T(8,128)}, u32[]{:S(2)}) copy-start(f32[4096,128]{1,0:T(8,128)} %get-tuple-element.609) | copy-start | bytes 6291460
  848.2 236.5 %reduce-scatter.5.cloned.1.call-start = ((), (), s32[]{:S(2)}) async-start(), calls=%async_computation.4 | async-start | bytes 1081344 | tf_op jit(solution)/shard_map/reduce_scatter | solution.py:199
  861.4 16.6 %collective-permute-start.18 = (bf16[4096,128]{1,0:T(8,128)(2,1)}, bf16[4096,128]{1,0:T(8,128)(2,1)S(1)}, u32[]{:S(2)}, u32[]{:S(2)}) collective-permute-start(bf16[4096,128]{1,0:T(8,128)(2,1)} %collective-permute-done.17), channel_id=1, source_target_pairs={{0,128},{32,160},{64,192},{96,224},{128,0},{160,32},{192,64},{224,... | collective-permute-start | bytes 3145736 | tf_op jit(solution)/shard_map/ppermute | solution.py:10
  861.5 26.7 %copy-start.11 = (u32[256]{0:T(256)S(1)}, u32[256]{0:T(256)}, u32[]{:S(2)}) copy-start(u32[256]{0:T(256)} %constant.306) | copy-start | bytes 3076
  879.3 5.2 collective-permute-start.13
  884.6 3.7 collective-permute-start.14
  888.2 5.2 collective-permute-start.15
  (70 other events, 220.5 us)
Sparse Core Ops, SparseCore 0:
  24.0 67.8 all-gather.2
  94.4 62.8 all-gather.4
  848.3 119.7 reduce-scatter.6
  970.5 114.1 reduce-scatter.4
where the time goes:
time: 1100 us; the launch traced here: 1090 us
  waiting for transfers between devices  374 us (34%)
  matrix products  304 us (28%)
  starting transfers between devices  181 us (16%)
  other arithmetic  108 us (10%)
  blocking collectives  91.4 us (8%)
  local copies, waits for them, and re-layouts  15.7 us (1%)
  between operations  14.6 us (1%)
    ppermute x36, starting transfers between devices, passed_along(): lax.ppermute(value, axis, [(source, source + steps) for source in range(i...  138 us
    dot_general x54, matrix products, apply_layer(): jnp.dot(reduced, second_weight, preferred_element_type=jnp.float32)  122 us
    ppermute x18, waiting for transfers between devices, partner(): lax.ppermute(shard, axis, [(i, i ^ 1 << distance) for i in range(lax.axis...  120 us
    reduce_scatter x1, waiting for transfers between devices, per_device(): lax.psum_scatter(pair_sums[1].astype(jnp.bfloat16), 'dp', scatter_dimensi...  115 us
    dot_general x72, matrix products, apply_layer(): jnp.einsum('hqk,khd->qhd', probabilities, split_heads, preferred_element_...  77 us
    dot_general x36, matrix products, apply_layer(): jnp.dot(mixed_heads, first_weight, preferred_element_type=jnp.float32)  69.7 us
    all_gather x1, waiting for transfers between devices, per_device(): lax.all_gather(stacked[1], 'dp', axis=1, tiled=True)  65.1 us
    ppermute x36, waiting for transfers between devices, passed_along(): lax.ppermute(value, axis, [(source, source + steps) for source in range(i...  54.4 us
  transfers between devices with their start and end apart: 58, of which 29 were waited for; matrix products, arithmetic and copies ran while one was open for 20% of the time, Pallas kernels for 0%

commit v1 on v0

--- a/solution.py
+++ b/solution.py
@@ -107,7 +107,9 @@
     )
     full_gain, full_first, full_second = (
         lax.all_gather(stacked[0], "dp", axis=1, tiled=True),
-        lax.all_gather(stacked[1], "dp", axis=1, tiled=True),
+        jnp.concatenate(
+            lax.all_to_all(jnp.stack([stacked[1]] * lax.axis_size("dp")), "dp", 0, 0), axis=1
+        ),
         lax.all_gather(stacked[2], "dp", axis=2, tiled=True),
     )
 

time: 1100 us -> 1060 us (0.964)
  waiting for transfers between devices: 374 us -> 304 us
  blocking collectives: 91.4 us -> 119 us
  local copies, waits for them, and re-layouts: 15.7 us -> 32.5 us
  other arithmetic: 108 us -> 94.3 us
    all_gather x1 -> x0, waiting for transfers between devices: 65.1 us -> none  [per_device(): lax.all_gather(stacked[1], 'dp', axis=1, tiled=True)]
    all_gather x1, blocking collectives: 37.2 us -> 64.8 us  [per_device(): lax.all_gather(stacked[0], 'dp', axis=1, tiled=True)]
  transfers between devices with their start and end apart: 58 -> 58, of which waited for: 29 -> 28; matrix products, arithmetic and copies ran while one was open for 20% -> 21% of each run, Pallas kernels for 0% -> 0%
where the time goes in v1:
time: 1060 us
  matrix products  306 us (29%)
  waiting for transfers between devices  304 us (29%)
  starting transfers between devices  185 us (17%)
  blocking collectives  119 us (11%)
  other arithmetic  94.3 us (9%)
  local copies, waits for them, and re-layouts  32.5 us (3%)
  between operations  14.6 us (1%)
    ppermute x36, starting transfers between devices, passed_along(): lax.ppermute(value, axis, [(source, source + steps) for source in range(i...  138 us
    dot_general x54, matrix products, apply_layer(): jnp.dot(reduced, second_weight, preferred_element_type=jnp.float32)  122 us
    reduce_scatter x1, waiting for transfers between devices, per_device(): lax.psum_scatter(pair_sums[1].astype(jnp.bfloat16), 'dp', scatter_dimensi...  115 us
    ppermute x18, waiting for transfers between devices, partner(): lax.ppermute(shard, axis, [(i, i ^ 1 << distance) for i in range(lax.axis...  112 us
    dot_general x72, matrix products, apply_layer(): jnp.einsum('hqk,khd->qhd', probabilities, split_heads, preferred_element_...  78.6 us
    dot_general x36, matrix products, apply_layer(): jnp.dot(mixed_heads, first_weight, preferred_element_type=jnp.float32)  69.8 us
    all_gather x1, blocking collectives, per_device(): lax.all_gather(stacked[0], 'dp', axis=1, tiled=True)  64.8 us
    ppermute x36, waiting for transfers between devices, passed_along(): lax.ppermute(value, axis, [(source, source + steps) for source in range(i...  54.9 us
  transfers between devices with their start and end apart: 58, of which 28 were waited for; matrix products, arithmetic and copies ran while one was open for 21% of the time, Pallas kernels for 0%

profile of v1, /device:TPU:2, one launch (start us, length us, event | category | flops | bytes accessed | tf_op | source)
XLA Modules:
  0.0 1059.6 jit_solution(1210736387638597345)
XLA Ops:
  25.5 9.5 all-to-all-start
  50.6 64.8 %all_gather.7 = bf16[2,4096]{1,0:T(2,128)(2,1)S(1)} all-gather(bf16[2,128]{1,0:T(2,128)(2,1)S(1)} %pad_maximum_fusion.2), channel_id=1, replica_groups=mesh['pipe'=8,'dp'=32] {'dp'}, dimensions={1}, use_global_device_ids=true | all-gather | bytes 16896 | tf_op jit(solution)/shard_map/all_gather | solution.py:109
  119.4 292.0 %while.49 = (s32[]{:T(128)}, bf16[32,4096]{1,0:T(8,128)(2,1)}, bf16[32,4096]{1,0:T(8,128)(2,1)}, bf16[2,2,32,4096]{3,2,1,0:T(8,128)(2,1)S(1)}, pred[]{:T(512)}, ...) while((s32[]{:T(128)}, bf16[32,4096]{1,0:T(8,128)(2,1)}, ...), condition=%wide.region_8.9_spmd, body=%wide.region_1.8_spmd.sunk | while | flops 172771520 | bytes 16375527 | solution.py:142
  131.4 5.1 collective-permute-start.1
  145.0 10.4 collective-permute-done
  176.4 5.4 collective-permute-start
  181.8 6.4 collective-permute-done
  209.1 5.4 collective-permute-start
  214.5 5.5 collective-permute-done
  240.9 5.4 collective-permute-start
  246.3 5.4 collective-permute-done
  272.7 5.4 collective-permute-start
  278.1 5.4 collective-permute-done
  304.5 5.4 collective-permute-start
  309.9 5.4 collective-permute-done
  336.2 5.4 collective-permute-start
  341.7 5.4 collective-permute-done
  368.0 5.4 collective-permute-start
  373.4 5.4 collective-permute-done
  399.8 5.4 collective-permute-start
  405.2 5.4 collective-permute-done
  412.8 318.1 %while.50 = (s32[]{:T(128)}, bf16[32,4096]{1,0:T(8,128)(2,1)}, bf16[32,4096]{1,0:T(8,128)(2,1)}, f32[4096]{0:T(1024)S(1)}, f32[4096,128]{1,0:T(8,128)}, /*index=...) while((s32[]{:T(128)}, bf16[32,4096]{1,0:T(8,128)(2,1)}, ...), condition=%wide.region_20.21_spmd.clone, body=%wide.region_9.20_spmd.clone.sunk | while | flops 456771968 | bytes 64646480 | solution.py:179
  424.5 5.4 collective-permute-start.3
  457.4 4.5 collective-permute-start.3
  465.1 3.8 fusion.335
  472.4 3.8 fusion.338
  489.6 3.7 collective-permute-start.2
  493.3 4.5 collective-permute-start.3
  500.9 3.8 fusion.335
  508.3 3.8 fusion.338
  525.4 3.7 collective-permute-start.2
  529.1 4.5 collective-permute-start.3
  536.8 3.8 fusion.335
  544.1 3.8 fusion.338
  561.3 3.7 collective-permute-start.2
  565.0 4.5 collective-permute-start.3
  572.7 3.8 fusion.335
  580.0 3.8 fusion.338
  597.2 3.7 collective-permute-start.2
  600.9 4.5 collective-permute-start.3
  608.6 3.8 fusion.335
  615.9 3.8 fusion.338
  633.0 3.7 collective-permute-start.2
  636.8 4.5 collective-permute-start.3
  644.4 3.8 fusion.335
  651.8 3.8 fusion.338
  672.6 4.5 collective-permute-start.3
  680.3 3.8 fusion.335
  687.6 3.8 fusion.338
  708.5 4.5 collective-permute-start.3
  716.2 3.8 fusion.335
  723.5 3.8 fusion.338
  732.7 4.7 collective-permute-start.19
  737.5 19.9 %collective-permute-done.19 = bf16[128,4096]{1,0:T(8,128)(2,1)S(1)} collective-permute-done((bf16[128,4096]{1,0:T(8,128)(2,1)S(1)}, bf16[128,4096]{1,0:T(8,128)(2,1)S(1)}, u32[]{:S(2)}, u32[]{:S(2)}) %collective-permute-start.19) | collective-permute-done | bytes 1048608 | tf_op jit(solution)/shard_map/ppermute | solution.py:10
  757.5 3.9 collective-permute-start.16
  761.4 22.0 %collective-permute-done.20 = bf16[128,4096]{1,0:T(8,128)(2,1)S(1)} collective-permute-done((bf16[128,4096]{1,0:T(8,128)(2,1)S(1)}, bf16[128,4096]{1,0:T(8,128)(2,1)S(1)}, u32[]{:S(2)}, u32[]{:S(2)}) %collective-permute-start.20) | collective-permute-done | bytes 1048608 | tf_op jit(solution)/shard_map/ppermute | solution.py:10
  783.4 7.6 collective-permute-start.21
  791.9 20.9 %collective-permute-done.21 = bf16[128,4096]{1,0:T(8,128)(2,1)S(1)} collective-permute-done((bf16[128,4096]{1,0:T(8,128)(2,1)S(1)}, bf16[128,4096]{1,0:T(8,128)(2,1)S(1)}, u32[]{:S(2)}, u32[]{:S(2)}) %collective-permute-start.21) | collective-permute-done | bytes 1048608 | tf_op jit(solution)/shard_map/ppermute | solution.py:10
  816.6 10.4 collective-permute-done.17
  827.1 16.5 %collective-permute-done.18 = bf16[4096,128]{1,0:T(8,128)(2,1)S(1)} collective-permute-done((bf16[4096,128]{1,0:T(8,128)(2,1)}, bf16[4096,128]{1,0:T(8,128)(2,1)S(1)}, u32[]{:S(2)}, u32[]{:S(2)}) %collective-permute-start.18) | collective-permute-done | bytes 1048608 | tf_op jit(solution)/shard_map/ppermute | solution.py:10
  855.1 3.9 collective-permute-done.15
  859.0 54.2 %all-reduce = bf16[4096]{0:T(1024)(128)(2,1)S(1)} all-reduce(bf16[4096]{0:T(1024)(128)(2,1)S(1)} %add_convert_fusion.2), channel_id=2, replica_groups=mesh['pipe'=8,'dp'=32] {'dp'}, use_global_device_ids=true, to_apply=%region_21.22.clone | all-reduce | flops 4096 | bytes 16384
  913.8 21.2 %reduce-scatter.7.cloned.1.call-done = bf16[128,128]{1,0:T(8,128)(2,1)} async-done(((bf16[4096,128]{1,0:T(8,128)(2,1)}), bf16[128,128]{1,0:T(8,128)(2,1)}) %reduce-scatter.7.cloned.1.call-update) | async-done | bytes 32784
  936.5 115.2 %reduce-scatter.5.cloned.1.call-done = bf16[128,128]{1,0:T(8,128)(2,1)} async-done(((bf16[4096,128]{1,0:T(8,128)(2,1)}), bf16[128,128]{1,0:T(8,128)(2,1)}) %reduce-scatter.5.cloned.1.call-update) | async-done | bytes 32784 | tf_op jit(solution)/shard_map/reduce_scatter | solution.py:201
  (760 shorter events, 442.3 us)
Async XLA Ops:
  7.2 5.7 collective-permute-start.7
  10.4 5.6 collective-permute-start.4
  12.9 4.6 collective-permute-start.8
  16.1 4.2 collective-permute-start.5
  17.5 5.4 collective-permute-start.9
  20.2 14.9 %collective-permute-start.6 = (bf16[1,128,128]{2,1,0:T(8,128)(2,1)S(1)}, bf16[1,128,128]{2,1,0:T(8,128)(2,1)S(1)}, u32[]{:S(2)}, u32[]{:S(2)}) collective-permute-start(bf16[1,128,128]{2,1,0:T(8,128)(2,1)S(1)} %collective-permute-done.5), channel_id=1, source_target_pairs={{0,128},{32,160},{64,192},{96,224},{128,0},{160,32},{192,64},{224,... | collective-permute-start | bytes 98312 | tf_op jit(solution)/shard_map/ppermute | solution.py:10
  25.5 13.4 %copy-start.13 = (s32[2,2]{1,0:T(2,128)S(1)}, s32[2,2]{1,0:T(2,128)}, u32[]{:S(2)}) copy-start(s32[2,2]{1,0:T(2,128)} %param.18) | copy-start | bytes 52
  25.5 13.5 %copy-start.12 = (s32[2,2,4]{2,1,0:T(2,128)S(1)}, s32[2,2,4]{2,1,0:T(2,128)}, u32[]{:S(2)}) copy-start(s32[2,2,4]{2,1,0:T(2,128)} %param.17) | copy-start | bytes 196
  25.5 89.9 %all-to-all-start = ((bf16[32,2,128,128]{3,2,1,0:T(8,128)(2,1)}), bf16[32,2,128,128]{3,2,1,0:T(8,128)(2,1)}, u32[]{:S(2)}, u32[]{:S(2)}) async-start(bf16[32,2,128,128]{3,2,1,0:T(8,128)(2,1)} %stack.2), calls=%async_computation | async-start | bytes 4194304 | tf_op jit(solution)/shard_map/all_to_all | solution.py:111
  35.1 82.8 %all-gather.2.cloned.1.call-start = ((), (), s32[]{:S(2)}) async-start(), calls=%async_computation.3 | async-start | bytes 2162688 | tf_op jit(solution)/shard_map/all_gather | solution.py:113
  35.8 899.2 %reduce-scatter.7.cloned.1.call-start = ((), (), s32[]{:S(2)}) async-start(), calls=%async_computation.5 | async-start | bytes 1081344
  35.9 6.1 collective-permute-start.10
  42.0 3.6 collective-permute-start.11
  45.5 5.1 collective-permute-start.12
  131.4 13.6 %collective-permute-start.1 = (bf16[32,4096]{1,0:T(8,128)(2,1)}, bf16[32,4096]{1,0:T(8,128)(2,1)}, u32[]{:S(2)}, u32[]{:S(2)}) collective-permute-start(bf16[32,4096]{1,0:T(8,128)(2,1)} %fusion.286), channel_id=1, source_target_pairs={{32,0},{64,32},{96,64},{128,96},{160,128},{192,160},{224,192},{33,... | collective-permute-start | bytes 786440 | tf_op jit(solution)/shard_map/while/body/eval_jaxpr/ppermute | solution.py:16
  142.8 12.7 %collective-permute-start = (bf16[32,4096]{1,0:T(8,128)(2,1)}, bf16[32,4096]{1,0:T(8,128)(2,1)S(1)}, u32[]{:S(2)}, u32[]{:S(2)}) collective-permute-start(bf16[32,4096]{1,0:T(8,128)(2,1)} %fusion.281), channel_id=1, source_target_pairs={{0,32},{32,64},{64,96},{96,128},{128,160},{160,192},{192,224},{1,3... | collective-permute-start | bytes 786440 | tf_op jit(solution)/shard_map/while/body/eval_jaxpr/ppermute | solution.py:16
  168.2 13.6 %collective-permute-start.1 = (bf16[32,4096]{1,0:T(8,128)(2,1)}, bf16[32,4096]{1,0:T(8,128)(2,1)}, u32[]{:S(2)}, u32[]{:S(2)}) collective-permute-start(bf16[32,4096]{1,0:T(8,128)(2,1)} %fusion.286), channel_id=1, source_target_pairs={{32,0},{64,32},{96,64},{128,96},{160,128},{192,160},{224,192},{33,... | collective-permute-start | bytes 786440 | tf_op jit(solution)/shard_map/while/body/eval_jaxpr/ppermute | solution.py:16
  176.4 11.8 %collective-permute-start = (bf16[32,4096]{1,0:T(8,128)(2,1)}, bf16[32,4096]{1,0:T(8,128)(2,1)S(1)}, u32[]{:S(2)}, u32[]{:S(2)}) collective-permute-start(bf16[32,4096]{1,0:T(8,128)(2,1)} %fusion.281), channel_id=1, source_target_pairs={{0,32},{32,64},{64,96},{96,128},{128,160},{160,192},{192,224},{1,3... | collective-permute-start | bytes 786440 | tf_op jit(solution)/shard_map/while/body/eval_jaxpr/ppermute | solution.py:16
  200.9 13.6 %collective-permute-start.1 = (bf16[32,4096]{1,0:T(8,128)(2,1)}, bf16[32,4096]{1,0:T(8,128)(2,1)}, u32[]{:S(2)}, u32[]{:S(2)}) collective-permute-start(bf16[32,4096]{1,0:T(8,128)(2,1)} %fusion.286), channel_id=1, source_target_pairs={{32,0},{64,32},{96,64},{128,96},{160,128},{192,160},{224,192},{33,... | collective-permute-start | bytes 786440 | tf_op jit(solution)/shard_map/while/body/eval_jaxpr/ppermute | solution.py:16
  209.1 10.9 %collective-permute-start = (bf16[32,4096]{1,0:T(8,128)(2,1)}, bf16[32,4096]{1,0:T(8,128)(2,1)S(1)}, u32[]{:S(2)}, u32[]{:S(2)}) collective-permute-start(bf16[32,4096]{1,0:T(8,128)(2,1)} %fusion.281), channel_id=1, source_target_pairs={{0,32},{32,64},{64,96},{96,128},{128,160},{160,192},{192,224},{1,3... | collective-permute-start | bytes 786440 | tf_op jit(solution)/shard_map/while/body/eval_jaxpr/ppermute | solution.py:16
  232.8 13.6 %collective-permute-start.1 = (bf16[32,4096]{1,0:T(8,128)(2,1)}, bf16[32,4096]{1,0:T(8,128)(2,1)}, u32[]{:S(2)}, u32[]{:S(2)}) collective-permute-start(bf16[32,4096]{1,0:T(8,128)(2,1)} %fusion.286), channel_id=1, source_target_pairs={{32,0},{64,32},{96,64},{128,96},{160,128},{192,160},{224,192},{33,... | collective-permute-start | bytes 786440 | tf_op jit(solution)/shard_map/while/body/eval_jaxpr/ppermute | solution.py:16
  240.9 10.9 %collective-permute-start = (bf16[32,4096]{1,0:T(8,128)(2,1)}, bf16[32,4096]{1,0:T(8,128)(2,1)S(1)}, u32[]{:S(2)}, u32[]{:S(2)}) collective-permute-start(bf16[32,4096]{1,0:T(8,128)(2,1)} %fusion.281), channel_id=1, source_target_pairs={{0,32},{32,64},{64,96},{96,128},{128,160},{160,192},{192,224},{1,3... | collective-permute-start | bytes 786440 | tf_op jit(solution)/shard_map/while/body/eval_jaxpr/ppermute | solution.py:16
  264.5 13.6 %collective-permute-start.1 = (bf16[32,4096]{1,0:T(8,128)(2,1)}, bf16[32,4096]{1,0:T(8,128)(2,1)}, u32[]{:S(2)}, u32[]{:S(2)}) collective-permute-start(bf16[32,4096]{1,0:T(8,128)(2,1)} %fusion.286), channel_id=1, source_target_pairs={{32,0},{64,32},{96,64},{128,96},{160,128},{192,160},{224,192},{33,... | collective-permute-start | bytes 786440 | tf_op jit(solution)/shard_map/while/body/eval_jaxpr/ppermute | solution.py:16
  272.7 10.9 %collective-permute-start = (bf16[32,4096]{1,0:T(8,128)(2,1)}, bf16[32,4096]{1,0:T(8,128)(2,1)S(1)}, u32[]{:S(2)}, u32[]{:S(2)}) collective-permute-start(bf16[32,4096]{1,0:T(8,128)(2,1)} %fusion.281), channel_id=1, source_target_pairs={{0,32},{32,64},{64,96},{96,128},{128,160},{160,192},{192,224},{1,3... | collective-permute-start | bytes 786440 | tf_op jit(solution)/shard_map/while/body/eval_jaxpr/ppermute | solution.py:16
  296.3 13.6 %collective-permute-start.1 = (bf16[32,4096]{1,0:T(8,128)(2,1)}, bf16[32,4096]{1,0:T(8,128)(2,1)}, u32[]{:S(2)}, u32[]{:S(2)}) collective-permute-start(bf16[32,4096]{1,0:T(8,128)(2,1)} %fusion.286), channel_id=1, source_target_pairs={{32,0},{64,32},{96,64},{128,96},{160,128},{192,160},{224,192},{33,... | collective-permute-start | bytes 786440 | tf_op jit(solution)/shard_map/while/body/eval_jaxpr/ppermute | solution.py:16
  304.5 10.9 %collective-permute-start = (bf16[32,4096]{1,0:T(8,128)(2,1)}, bf16[32,4096]{1,0:T(8,128)(2,1)S(1)}, u32[]{:S(2)}, u32[]{:S(2)}) collective-permute-start(bf16[32,4096]{1,0:T(8,128)(2,1)} %fusion.281), channel_id=1, source_target_pairs={{0,32},{32,64},{64,96},{96,128},{128,160},{160,192},{192,224},{1,3... | collective-permute-start | bytes 786440 | tf_op jit(solution)/shard_map/while/body/eval_jaxpr/ppermute | solution.py:16
  328.1 13.6 %collective-permute-start.1 = (bf16[32,4096]{1,0:T(8,128)(2,1)}, bf16[32,4096]{1,0:T(8,128)(2,1)}, u32[]{:S(2)}, u32[]{:S(2)}) collective-permute-start(bf16[32,4096]{1,0:T(8,128)(2,1)} %fusion.286), channel_id=1, source_target_pairs={{32,0},{64,32},{96,64},{128,96},{160,128},{192,160},{224,192},{33,... | collective-permute-start | bytes 786440 | tf_op jit(solution)/shard_map/while/body/eval_jaxpr/ppermute | solution.py:16
  336.2 10.9 %collective-permute-start = (bf16[32,4096]{1,0:T(8,128)(2,1)}, bf16[32,4096]{1,0:T(8,128)(2,1)S(1)}, u32[]{:S(2)}, u32[]{:S(2)}) collective-permute-start(bf16[32,4096]{1,0:T(8,128)(2,1)} %fusion.281), channel_id=1, source_target_pairs={{0,32},{32,64},{64,96},{96,128},{128,160},{160,192},{192,224},{1,3... | collective-permute-start | bytes 786440 | tf_op jit(solution)/shard_map/while/body/eval_jaxpr/ppermute | solution.py:16
  359.9 13.6 %collective-permute-start.1 = (bf16[32,4096]{1,0:T(8,128)(2,1)}, bf16[32,4096]{1,0:T(8,128)(2,1)}, u32[]{:S(2)}, u32[]{:S(2)}) collective-permute-start(bf16[32,4096]{1,0:T(8,128)(2,1)} %fusion.286), channel_id=1, source_target_pairs={{32,0},{64,32},{96,64},{128,96},{160,128},{192,160},{224,192},{33,... | collective-permute-start | bytes 786440 | tf_op jit(solution)/shard_map/while/body/eval_jaxpr/ppermute | solution.py:16
  368.0 10.9 %collective-permute-start = (bf16[32,4096]{1,0:T(8,128)(2,1)}, bf16[32,4096]{1,0:T(8,128)(2,1)S(1)}, u32[]{:S(2)}, u32[]{:S(2)}) collective-permute-start(bf16[32,4096]{1,0:T(8,128)(2,1)} %fusion.281), channel_id=1, source_target_pairs={{0,32},{32,64},{64,96},{96,128},{128,160},{160,192},{192,224},{1,3... | collective-permute-start | bytes 786440 | tf_op jit(solution)/shard_map/while/body/eval_jaxpr/ppermute | solution.py:16
  391.7 13.6 %collective-permute-start.1 = (bf16[32,4096]{1,0:T(8,128)(2,1)}, bf16[32,4096]{1,0:T(8,128)(2,1)}, u32[]{:S(2)}, u32[]{:S(2)}) collective-permute-start(bf16[32,4096]{1,0:T(8,128)(2,1)} %fusion.286), channel_id=1, source_target_pairs={{32,0},{64,32},{96,64},{128,96},{160,128},{192,160},{224,192},{33,... | collective-permute-start | bytes 786440 | tf_op jit(solution)/shard_map/while/body/eval_jaxpr/ppermute | solution.py:16
  399.8 10.9 %collective-permute-start = (bf16[32,4096]{1,0:T(8,128)(2,1)}, bf16[32,4096]{1,0:T(8,128)(2,1)S(1)}, u32[]{:S(2)}, u32[]{:S(2)}) collective-permute-start(bf16[32,4096]{1,0:T(8,128)(2,1)} %fusion.281), channel_id=1, source_target_pairs={{0,32},{32,64},{64,96},{96,128},{128,160},{160,192},{192,224},{1,3... | collective-permute-start | bytes 786440 | tf_op jit(solution)/shard_map/while/body/eval_jaxpr/ppermute | solution.py:16
  422.6 22.2 %collective-permute-start.2 = (bf16[32,4096]{1,0:T(8,128)(2,1)}, bf16[32,4096]{1,0:T(8,128)(2,1)}, u32[]{:S(2)}, u32[]{:S(2)}) collective-permute-start(bf16[32,4096]{1,0:T(8,128)(2,1)} %fusion.332), channel_id=1, source_target_pairs={{32,0},{64,32},{96,64},{128,96},{160,128},{192,160},{224,192},{33,... | collective-permute-start | bytes 786440 | tf_op jit(solution)/shard_map/while/body/eval_jaxpr/ppermute | solution.py:16
  424.5 20.3 %collective-permute-start.3 = (bf16[32,4096]{1,0:T(8,128)(2,1)}, bf16[32,4096]{1,0:T(8,128)(2,1)}, u32[]{:S(2)}, u32[]{:S(2)}) collective-permute-start(bf16[32,4096]{1,0:T(8,128)(2,1)} %get-tuple-element.1028), channel_id=1, source_target_pairs={{0,32},{32,64},{64,96},{96,128},{128,160},{160,192},{192,224},{1,3... | collective-permute-start | bytes 786440 | tf_op jit(solution)/shard_map/while/body/eval_jaxpr/ppermute | solution.py:16
  454.6 25.1 %collective-permute-start.2 = (bf16[32,4096]{1,0:T(8,128)(2,1)}, bf16[32,4096]{1,0:T(8,128)(2,1)}, u32[]{:S(2)}, u32[]{:S(2)}) collective-permute-start(bf16[32,4096]{1,0:T(8,128)(2,1)} %fusion.332), channel_id=1, source_target_pairs={{32,0},{64,32},{96,64},{128,96},{160,128},{192,160},{224,192},{33,... | collective-permute-start | bytes 786440 | tf_op jit(solution)/shard_map/while/body/eval_jaxpr/ppermute | solution.py:16
  457.4 22.3 %collective-permute-start.3 = (bf16[32,4096]{1,0:T(8,128)(2,1)}, bf16[32,4096]{1,0:T(8,128)(2,1)}, u32[]{:S(2)}, u32[]{:S(2)}) collective-permute-start(bf16[32,4096]{1,0:T(8,128)(2,1)} %get-tuple-element.1028), channel_id=1, source_target_pairs={{0,32},{32,64},{64,96},{96,128},{128,160},{160,192},{192,224},{1,3... | collective-permute-start | bytes 786440 | tf_op jit(solution)/shard_map/while/body/eval_jaxpr/ppermute | solution.py:16
  489.6 26.0 %collective-permute-start.2 = (bf16[32,4096]{1,0:T(8,128)(2,1)}, bf16[32,4096]{1,0:T(8,128)(2,1)}, u32[]{:S(2)}, u32[]{:S(2)}) collective-permute-start(bf16[32,4096]{1,0:T(8,128)(2,1)} %fusion.332), channel_id=1, source_target_pairs={{32,0},{64,32},{96,64},{128,96},{160,128},{192,160},{224,192},{33,... | collective-permute-start | bytes 786440 | tf_op jit(solution)/shard_map/while/body/eval_jaxpr/ppermute | solution.py:16
  493.3 22.3 %collective-permute-start.3 = (bf16[32,4096]{1,0:T(8,128)(2,1)}, bf16[32,4096]{1,0:T(8,128)(2,1)}, u32[]{:S(2)}, u32[]{:S(2)}) collective-permute-start(bf16[32,4096]{1,0:T(8,128)(2,1)} %get-tuple-element.1028), channel_id=1, source_target_pairs={{0,32},{32,64},{64,96},{96,128},{128,160},{160,192},{192,224},{1,3... | collective-permute-start | bytes 786440 | tf_op jit(solution)/shard_map/while/body/eval_jaxpr/ppermute | solution.py:16
  525.4 26.0 %collective-permute-start.2 = (bf16[32,4096]{1,0:T(8,128)(2,1)}, bf16[32,4096]{1,0:T(8,128)(2,1)}, u32[]{:S(2)}, u32[]{:S(2)}) collective-permute-start(bf16[32,4096]{1,0:T(8,128)(2,1)} %fusion.332), channel_id=1, source_target_pairs={{32,0},{64,32},{96,64},{128,96},{160,128},{192,160},{224,192},{33,... | collective-permute-start | bytes 786440 | tf_op jit(solution)/shard_map/while/body/eval_jaxpr/ppermute | solution.py:16
  529.1 22.3 %collective-permute-start.3 = (bf16[32,4096]{1,0:T(8,128)(2,1)}, bf16[32,4096]{1,0:T(8,128)(2,1)}, u32[]{:S(2)}, u32[]{:S(2)}) collective-permute-start(bf16[32,4096]{1,0:T(8,128)(2,1)} %get-tuple-element.1028), channel_id=1, source_target_pairs={{0,32},{32,64},{64,96},{96,128},{128,160},{160,192},{192,224},{1,3... | collective-permute-start | bytes 786440 | tf_op jit(solution)/shard_map/while/body/eval_jaxpr/ppermute | solution.py:16
  561.3 26.0 %collective-permute-start.2 = (bf16[32,4096]{1,0:T(8,128)(2,1)}, bf16[32,4096]{1,0:T(8,128)(2,1)}, u32[]{:S(2)}, u32[]{:S(2)}) collective-permute-start(bf16[32,4096]{1,0:T(8,128)(2,1)} %fusion.332), channel_id=1, source_target_pairs={{32,0},{64,32},{96,64},{128,96},{160,128},{192,160},{224,192},{33,... | collective-permute-start | bytes 786440 | tf_op jit(solution)/shard_map/while/body/eval_jaxpr/ppermute | solution.py:16
  565.0 22.3 %collective-permute-start.3 = (bf16[32,4096]{1,0:T(8,128)(2,1)}, bf16[32,4096]{1,0:T(8,128)(2,1)}, u32[]{:S(2)}, u32[]{:S(2)}) collective-permute-start(bf16[32,4096]{1,0:T(8,128)(2,1)} %get-tuple-element.1028), channel_id=1, source_target_pairs={{0,32},{32,64},{64,96},{96,128},{128,160},{160,192},{192,224},{1,3... | collective-permute-start | bytes 786440 | tf_op jit(solution)/shard_map/while/body/eval_jaxpr/ppermute | solution.py:16
  597.2 26.0 %collective-permute-start.2 = (bf16[32,4096]{1,0:T(8,128)(2,1)}, bf16[32,4096]{1,0:T(8,128)(2,1)}, u32[]{:S(2)}, u32[]{:S(2)}) collective-permute-start(bf16[32,4096]{1,0:T(8,128)(2,1)} %fusion.332), channel_id=1, source_target_pairs={{32,0},{64,32},{96,64},{128,96},{160,128},{192,160},{224,192},{33,... | collective-permute-start | bytes 786440 | tf_op jit(solution)/shard_map/while/body/eval_jaxpr/ppermute | solution.py:16
  600.9 22.3 %collective-permute-start.3 = (bf16[32,4096]{1,0:T(8,128)(2,1)}, bf16[32,4096]{1,0:T(8,128)(2,1)}, u32[]{:S(2)}, u32[]{:S(2)}) collective-permute-start(bf16[32,4096]{1,0:T(8,128)(2,1)} %get-tuple-element.1028), channel_id=1, source_target_pairs={{0,32},{32,64},{64,96},{96,128},{128,160},{160,192},{192,224},{1,3... | collective-permute-start | bytes 786440 | tf_op jit(solution)/shard_map/while/body/eval_jaxpr/ppermute | solution.py:16
  633.0 26.0 %collective-permute-start.2 = (bf16[32,4096]{1,0:T(8,128)(2,1)}, bf16[32,4096]{1,0:T(8,128)(2,1)}, u32[]{:S(2)}, u32[]{:S(2)}) collective-permute-start(bf16[32,4096]{1,0:T(8,128)(2,1)} %fusion.332), channel_id=1, source_target_pairs={{32,0},{64,32},{96,64},{128,96},{160,128},{192,160},{224,192},{33,... | collective-permute-start | bytes 786440 | tf_op jit(solution)/shard_map/while/body/eval_jaxpr/ppermute | solution.py:16
  636.8 22.3 %collective-permute-start.3 = (bf16[32,4096]{1,0:T(8,128)(2,1)}, bf16[32,4096]{1,0:T(8,128)(2,1)}, u32[]{:S(2)}, u32[]{:S(2)}) collective-permute-start(bf16[32,4096]{1,0:T(8,128)(2,1)} %get-tuple-element.1028), channel_id=1, source_target_pairs={{0,32},{32,64},{64,96},{96,128},{128,160},{160,192},{192,224},{1,3... | collective-permute-start | bytes 786440 | tf_op jit(solution)/shard_map/while/body/eval_jaxpr/ppermute | solution.py:16
  668.9 26.0 %collective-permute-start.2 = (bf16[32,4096]{1,0:T(8,128)(2,1)}, bf16[32,4096]{1,0:T(8,128)(2,1)}, u32[]{:S(2)}, u32[]{:S(2)}) collective-permute-start(bf16[32,4096]{1,0:T(8,128)(2,1)} %fusion.332), channel_id=1, source_target_pairs={{32,0},{64,32},{96,64},{128,96},{160,128},{192,160},{224,192},{33,... | collective-permute-start | bytes 786440 | tf_op jit(solution)/shard_map/while/body/eval_jaxpr/ppermute | solution.py:16
  672.6 22.3 %collective-permute-start.3 = (bf16[32,4096]{1,0:T(8,128)(2,1)}, bf16[32,4096]{1,0:T(8,128)(2,1)}, u32[]{:S(2)}, u32[]{:S(2)}) collective-permute-start(bf16[32,4096]{1,0:T(8,128)(2,1)} %get-tuple-element.1028), channel_id=1, source_target_pairs={{0,32},{32,64},{64,96},{96,128},{128,160},{160,192},{192,224},{1,3... | collective-permute-start | bytes 786440 | tf_op jit(solution)/shard_map/while/body/eval_jaxpr/ppermute | solution.py:16
  704.8 26.0 %collective-permute-start.2 = (bf16[32,4096]{1,0:T(8,128)(2,1)}, bf16[32,4096]{1,0:T(8,128)(2,1)}, u32[]{:S(2)}, u32[]{:S(2)}) collective-permute-start(bf16[32,4096]{1,0:T(8,128)(2,1)} %fusion.332), channel_id=1, source_target_pairs={{32,0},{64,32},{96,64},{128,96},{160,128},{192,160},{224,192},{33,... | collective-permute-start | bytes 786440 | tf_op jit(solution)/shard_map/while/body/eval_jaxpr/ppermute | solution.py:16
  708.5 22.3 %collective-permute-start.3 = (bf16[32,4096]{1,0:T(8,128)(2,1)}, bf16[32,4096]{1,0:T(8,128)(2,1)}, u32[]{:S(2)}, u32[]{:S(2)}) collective-permute-start(bf16[32,4096]{1,0:T(8,128)(2,1)} %get-tuple-element.1028), channel_id=1, source_target_pairs={{0,32},{32,64},{64,96},{96,128},{128,160},{160,192},{192,224},{1,3... | collective-permute-start | bytes 786440 | tf_op jit(solution)/shard_map/while/body/eval_jaxpr/ppermute | solution.py:16
  730.9 26.5 %copy-start.5 = (f32[4096,128]{1,0:T(8,128)S(1)}, f32[4096,128]{1,0:T(8,128)}, u32[]{:S(2)}) copy-start(f32[4096,128]{1,0:T(8,128)} %get-tuple-element.610) | copy-start | bytes 6291460
  732.7 58.3 %copy-start.3 = (f32[128,4096]{1,0:T(8,128)S(1)}, f32[128,4096]{1,0:T(8,128)}, u32[]{:S(2)}) copy-start(f32[128,4096]{1,0:T(8,128)} %get-tuple-element.611) | copy-start | bytes 6291460
  732.7 24.6 %collective-permute-start.19 = (bf16[128,4096]{1,0:T(8,128)(2,1)S(1)}, bf16[128,4096]{1,0:T(8,128)(2,1)S(1)}, u32[]{:S(2)}, u32[]{:S(2)}) collective-permute-start(bf16[128,4096]{1,0:T(8,128)(2,1)S(1)} %convert_element_type.624), channel_id=1, source_target_pairs={{0,32},{32,0},{64,96},{96,64},{128,160},{160,128},{192,224},{224,1... | collective-permute-start | bytes 3145736 | tf_op jit(solution)/shard_map/ppermute | solution.py:10
  757.4 26.0 %collective-permute-start.20 = (bf16[128,4096]{1,0:T(8,128)(2,1)S(1)}, bf16[128,4096]{1,0:T(8,128)(2,1)S(1)}, u32[]{:S(2)}, u32[]{:S(2)}) collective-permute-start(bf16[128,4096]{1,0:T(8,128)(2,1)S(1)} %collective-permute-done.19), channel_id=1, source_target_pairs={{0,64},{32,96},{64,0},{96,32},{128,192},{160,224},{192,128},{224,1... | collective-permute-start | bytes 3145736 | tf_op jit(solution)/shard_map/ppermute | solution.py:10
  757.5 33.7 %collective-permute-start.16 = (bf16[4096,128]{1,0:T(8,128)(2,1)S(1)}, bf16[4096,128]{1,0:T(8,128)(2,1)}, u32[]{:S(2)}, u32[]{:S(2)}) collective-permute-start(bf16[4096,128]{1,0:T(8,128)(2,1)S(1)} %convert_element_type.619), channel_id=1, source_target_pairs={{0,32},{32,0},{64,96},{96,64},{128,160},{160,128},{192,224},{224,1... | collective-permute-start | bytes 3145736 | tf_op jit(solution)/shard_map/ppermute | solution.py:10
  783.4 29.4 %collective-permute-start.21 = (bf16[128,4096]{1,0:T(8,128)(2,1)S(1)}, bf16[128,4096]{1,0:T(8,128)(2,1)S(1)}, u32[]{:S(2)}, u32[]{:S(2)}) collective-permute-start(bf16[128,4096]{1,0:T(8,128)(2,1)S(1)} %collective-permute-done.20), channel_id=1, source_target_pairs={{0,128},{32,160},{64,192},{96,224},{128,0},{160,32},{192,64},{224,... | collective-permute-start | bytes 3145736 | tf_op jit(solution)/shard_map/ppermute | solution.py:10
  791.2 35.8 %collective-permute-start.17 = (bf16[4096,128]{1,0:T(8,128)(2,1)}, bf16[4096,128]{1,0:T(8,128)(2,1)}, u32[]{:S(2)}, u32[]{:S(2)}) collective-permute-start(bf16[4096,128]{1,0:T(8,128)(2,1)} %collective-permute-done.16), channel_id=1, source_target_pairs={{0,64},{32,96},{64,0},{96,32},{128,192},{160,224},{192,128},{224,1... | collective-permute-start | bytes 3145736 | tf_op jit(solution)/shard_map/ppermute | solution.py:10
  814.1 12.9 %copy-start.4 = (f32[4096,128]{1,0:T(8,128)S(1)}, f32[4096,128]{1,0:T(8,128)}, u32[]{:S(2)}) copy-start(f32[4096,128]{1,0:T(8,128)} %get-tuple-element.609) | copy-start | bytes 6291460
  816.5 235.1 %reduce-scatter.5.cloned.1.call-start = ((), (), s32[]{:S(2)}) async-start(), calls=%async_computation.4 | async-start | bytes 1081344 | tf_op jit(solution)/shard_map/reduce_scatter | solution.py:201
  827.0 16.6 %collective-permute-start.18 = (bf16[4096,128]{1,0:T(8,128)(2,1)}, bf16[4096,128]{1,0:T(8,128)(2,1)S(1)}, u32[]{:S(2)}, u32[]{:S(2)}) collective-permute-start(bf16[4096,128]{1,0:T(8,128)(2,1)} %collective-permute-done.17), channel_id=1, source_target_pairs={{0,128},{32,160},{64,192},{96,224},{128,0},{160,32},{192,64},{224,... | collective-permute-start | bytes 3145736 | tf_op jit(solution)/shard_map/ppermute | solution.py:10
  827.1 26.7 %copy-start.15 = (u32[256]{0:T(256)S(1)}, u32[256]{0:T(256)}, u32[]{:S(2)}) copy-start(u32[256]{0:T(256)} %constant.306) | copy-start | bytes 3076
  844.9 5.2 collective-permute-start.13
  850.2 3.7 collective-permute-start.14
  853.8 5.2 collective-permute-start.15
  (66 other events, 184.6 us)
Sparse Core Ops, SparseCore 0:
  38.2 79.5 all-gather.1
  816.6 118.2 reduce-scatter.6
  937.5 114.1 reduce-scatter.4
